TPU v7x, 32 devices: a whole 2x2x4 slice. The times are simulated.
32 devices in a mesh: ens: 2 (over y), space: 4 (over z), tm: 2 (over x), mom: 2 (over core).
Axes of the slice: x: 2, y: 2, z: 4, core: 2. Of those that a mesh axis runs over, the one named last changes fastest.
Arguments:
- eigvecs: bfloat16 [8, 2, 3, 256, 2048], P(('ens', 'tm'), None, None, None, 'space'), parts along dimension 0, may hold values from -0.359375 to 0.359375
- momenta: int32 [4, 3], P('mom'), may hold values from 1 to 2
- pairs: int32 [2, 2], replicated, may hold values from 0 to 3, as said below
- spin_weights: float32 [4, 4], replicated, may hold values from -1 to 1
- perambulators: bfloat16 [4, 2, 4, 4, 256, 256], P(('ens', 'tm'), None, None, None, 'space'), parts along dimension 0, may hold values from -0.0234375 to 0.0234375
Outputs:
- blocks: bfloat16 [4, 4, 2, 256, 256], P(('ens', 'tm'), 'mom', None, 'space'), parts along dimension 0
There are 2 independent parts, one for each index of `ens`. A program takes and returns all parts, laid end to end along the dimension named above; an argument that names none is the same for every part. Nothing has to cross between parts.
Inputs may be any that keep to these rules, and one draw needn't show every extreme that they name: pairs[q, 0], the sink, lies in time group q: (q) * 2 <= pairs[q, 0] < (q + 1) * 2; pairs[q, 1], the source, is any timeslice.
All inputs are finite; a program needn't handle non-finite values.
Results may differ from a plain program's by a relative error of at most 0.008.
Values may be sent and summed in bfloat16 or wider, within the bound.
No kernel may reach another device: no remote copies, remote signals or barrier semaphores. Data moves between devices by JAX's collectives and lax.ppermute only.
A program may use at most 64 MiB of HBM per device.

v0:
```python
import math
import jax
import jax.numpy as jnp
from jax import lax
from jax.sharding import PartitionSpec as P

LAT = 48
EXACT_PRECISION = lax.Precision.HIGHEST


def phases(momenta, site_ids):
    xcoord = (site_ids % LAT).astype(jnp.float32)
    ycoord = (site_ids // LAT % LAT).astype(jnp.float32)
    zcoord = (site_ids // (LAT * LAT)).astype(jnp.float32)
    mom_float = momenta.astype(jnp.float32)
    angles = (
        mom_float[:, 0:1] * xcoord + mom_float[:, 1:2] * ycoord + mom_float[:, 2:3] * zcoord
    ) * (2.0 * math.pi / LAT)
    return (jnp.cos(angles), jnp.sin(angles))


def elemental_terms(eigvecs, cosine_rows, sine_rows):
    contract_dims = (((0, 2), (0, 2)), ((), ()))
    per_time = []
    for which_time in range(eigvecs.shape[0]):
        real_vec = eigvecs[which_time, 0]
        imag_vec = eigvecs[which_time, 1]
        real_wide = real_vec.astype(jnp.float32)
        imag_wide = imag_vec.astype(jnp.float32)
        per_mom = []
        for which_mom in range(cosine_rows.shape[0]):
            cosine = cosine_rows[which_mom]
            sine = sine_rows[which_mom]
            real_turned = (cosine * real_wide + sine * imag_wide).astype(jnp.bfloat16)
            imag_turned = (cosine * imag_wide - sine * real_wide).astype(jnp.bfloat16)
            real_part = lax.dot_general(
                real_vec, real_turned, contract_dims, preferred_element_type=jnp.float32
            ) + lax.dot_general(
                imag_vec, imag_turned, contract_dims, preferred_element_type=jnp.float32
            )
            imag_part = lax.dot_general(
                real_vec, imag_turned, contract_dims, preferred_element_type=jnp.float32
            ) - lax.dot_general(
                imag_vec, real_turned, contract_dims, preferred_element_type=jnp.float32
            )
            per_mom.append(jnp.stack([real_part, imag_part]))
        per_time.append(jnp.stack(per_mom))
    return jnp.stack(per_time)


def source_slots(held_rows, pairs, my_group, times_dev, tm_size, pair_dev):
    wanted = pairs[:, 1].reshape(tm_size, pair_dev)
    local_times = jnp.arange(times_dev, dtype=jnp.int32) + my_group * times_dev
    chosen = (wanted[:, :, None] == local_times).astype(jnp.bfloat16)
    return jnp.einsum(
        "rqt,tmcij->rqmcij", chosen, held_rows, preferred_element_type=jnp.float32
    ).astype(jnp.bfloat16)


def sink_select(held_rows, my_pairs, my_group, times_dev):
    local_times = jnp.arange(times_dev, dtype=jnp.int32) + my_group * times_dev
    chosen = (my_pairs[:, 0][:, None] == local_times).astype(jnp.bfloat16)
    return jnp.einsum(
        "qt,tmcij->qmcij", chosen, held_rows, preferred_element_type=jnp.float32
    ).astype(jnp.bfloat16)


def bridge(mixed_block, source):
    real_part = jnp.einsum(
        "qkl,qmjl->qmkj", mixed_block[:, 0], source[:, :, 0], preferred_element_type=jnp.float32
    ) + jnp.einsum(
        "qkl,qmjl->qmkj", mixed_block[:, 1], source[:, :, 1], preferred_element_type=jnp.float32
    )
    imag_part = jnp.einsum(
        "qkl,qmjl->qmkj", mixed_block[:, 1], source[:, :, 0], preferred_element_type=jnp.float32
    ) - jnp.einsum(
        "qkl,qmjl->qmkj", mixed_block[:, 0], source[:, :, 1], preferred_element_type=jnp.float32
    )
    return jnp.stack([real_part, imag_part], 2).astype(jnp.bfloat16)


def attach(sink_elem, bridged):
    real_part = jnp.einsum(
        "qmik,qmkj->qmij", sink_elem[:, :, 0], bridged[:, :, 0], preferred_element_type=jnp.float32
    ) - jnp.einsum(
        "qmik,qmkj->qmij", sink_elem[:, :, 1], bridged[:, :, 1], preferred_element_type=jnp.float32
    )
    imag_part = jnp.einsum(
        "qmik,qmkj->qmij", sink_elem[:, :, 0], bridged[:, :, 1], preferred_element_type=jnp.float32
    ) + jnp.einsum(
        "qmik,qmkj->qmij", sink_elem[:, :, 1], bridged[:, :, 0], preferred_element_type=jnp.float32
    )
    return jnp.stack([real_part, imag_part], 2)


def local(eigvecs, momenta, pairs, spin_weights, perambulators):
    times_dev = eigvecs.shape[0]
    vec_count = eigvecs.shape[3]
    sites_dev = eigvecs.shape[4]
    pair_dev = perambulators.shape[0]
    tm_size = lax.axis_size("tm")
    space_size = lax.axis_size("space")
    my_group = lax.axis_index("tm")
    my_place = lax.axis_index("space")
    rows_dev = vec_count // space_size
    row_first = my_place * rows_dev
    site_ids = my_place * sites_dev + jnp.arange(sites_dev, dtype=jnp.int32)
    cosine_rows, sine_rows = phases(momenta, site_ids)
    partial_value = elemental_terms(eigvecs, cosine_rows, sine_rows)
    my_pairs = lax.dynamic_slice_in_dim(pairs, my_group * pair_dev, pair_dev, 0)
    whole = lax.psum(partial_value, "space").astype(jnp.bfloat16)
    outgoing = source_slots(whole, pairs, my_group, times_dev, tm_size, pair_dev)
    arrived = lax.all_to_all(outgoing, "tm", split_axis=0, concat_axis=0, tiled=True)
    source_full = jnp.sum(arrived, axis=0, dtype=jnp.float32).astype(jnp.bfloat16)
    sink_whole = sink_select(whole, my_pairs, my_group, times_dev)
    sink_own = lax.dynamic_slice_in_dim(sink_whole, row_first, rows_dev, 3)
    mixed_peramb = jnp.einsum(
        "ab,qcabkl->qckl",
        spin_weights,
        perambulators.astype(jnp.float32),
        precision=EXACT_PRECISION,
    ).astype(jnp.bfloat16)
    bridged = bridge(lax.all_gather(mixed_peramb, "space", axis=2, tiled=True), source_full)
    blocks = attach(sink_own, bridged).astype(jnp.bfloat16)
    return blocks


def solution(mesh):
    return jax.shard_map(
        local,
        mesh=mesh,
        in_specs=(
            P(("ens", "tm"), None, None, None, "space"),
            P("mom", None),
            P(),
            P(),
            P(("ens", "tm"), None, None, None, "space", None),
        ),
        out_specs=P(("ens", "tm"), "mom", None, "space", None),
        check_vma=False,
    )
```

profile of v0, /device:TPU:0, one launch (start us, length us, event | category | flops | bytes accessed | tf_op | source)
XLA Modules:
  0.0 120.1 jit_solution(8111220607492806430)
XLA Ops:
  0.0 0.0 copy-start
  0.0 0.8 convert_element_type.166
  0.8 0.2 slice_reduce_fusion.3
  1.0 0.1 fusion.149
  1.1 0.1 sin.3
  1.3 0.0 copy-start.1
  1.3 2.2 %convolution_bitcast_fusion.14 = f32[256,256]{1,0:T(8,128)S(1)} fusion(f32[512]{0:T(512)S(1)} %bitcast.288, f32[512]{0:T(512)S(1)} %bitcast.296, bf16[2,2,3,256,512]{4,3,2,1,0:T(8,128)(2,1)} %param.5), kind=kOutput, calls=%fused_computation.55 | convolution fusion | flops 203685888 | bytes 2625536 | tf_op jit(solution)/shard_map/dot_general | solution.py:38
  3.5 0.4 copy-done.1
  3.9 0.4 convolution_bitcast_fusion.12
  4.3 0.5 convolution_bitcast_fusion.10
  4.8 0.4 convolution_bitcast_fusion.8
  5.2 0.4 convolution_bitcast_fusion.6
  5.7 0.5 convolution_bitcast_fusion.4
  6.1 0.5 convolution_bitcast_fusion.2
  6.6 0.4 convolution_bitcast_fusion
  7.1 0.4 fusion.22
  7.5 0.5 fusion.24
  8.0 0.5 fusion.26
  8.4 0.5 fusion.28
  8.9 0.5 fusion.30
  9.4 0.5 fusion.32
  9.8 0.5 fusion.34
  10.3 0.5 fusion.36
  10.8 0.1 maximum_bitcast_fusion
  11.0 0.1 maximum_bitcast_fusion.1
  11.1 0.1 pad_maximum_fusion
  11.2 79.3 %all-reduce.1 = bf16[2,2,2,256,256]{3,4,2,1,0:T(8,128)(2,1)} all-reduce(f32[2,2,2,256,256]{3,4,2,1,0:T(8,128)S(1)} %pad_maximum_fusion), channel_id=1, replica_groups=mesh['ens'=2,'space'=4,'tm'=2,'mom'=2] {'space'}, use_global_device_ids=true, to_apply=%region_0.1 | all-reduce | flops 524288 | bytes 3145728 | tf_op jit(solution)/shard_map/psum | solution.py:111
  90.5 0.0 copy-start.3
  90.5 2.5 %copy.12 = bf16[2,2,2,256,256]{4,0,3,2,1:T(2,128)(2,1)S(1)} copy(bf16[2,2,2,256,256]{3,4,2,1,0:T(8,128)(2,1)} %all-reduce.1) | data formatting | bytes 2097152 | tf_op jit(solution)/shard_map/convert_element_type | solution.py:111
  93.1 0.0 copy-done.3
  93.1 0.2 slice_reduce_fusion
  93.3 1.3 %fusion.16 = bf16[2,1,2,2,256,256]{5,0,4,3,2,1:T(2,128)(2,1)S(1)} fusion(bf16[2,2,2,256,256]{4,0,3,2,1:T(2,128)(2,1)S(1)} %copy.12, s32[2]{0:T(128)S(1)} %iota_add_fusion.1, s32[2]{0:T(128)S(1)} %slice_reduce_fusion), kind=kOutput, calls=%fused_computation.34 | convolution fusion | flops 2621444 | bytes 2097168 | tf_op jit(solution)/shard_map/rqt,tmcij->rqmcij/dot_general | solution.py:55
  94.6 1.1 copy.13
  95.7 0.0 copy-start.2
  95.7 3.9 %all-to-all-start = ((bf16[2,1,2,2,256,256]{5,4,3,2,1,0:T(8,128)(2,1)}), bf16[2,1,2,2,256,256]{5,4,3,2,1,0:T(8,128)(2,1)S(1)}, u32[]{:S(2)}, u32[]{:S(2)}) async-start(bf16[2,1,2,2,256,256]{5,4,3,2,1,0:T(8,128)(2,1)} %copy.13), calls=%async_computation | async-start | bytes 2097152 | tf_op jit(solution)/shard_map/all_to_all | solution.py:113
  99.6 0.0 copy-done
  99.6 0.0 copy-done.2
  99.6 2.1 %fusion.41 = bf16[1,2,64,256,1]{3,0,4,2,1:T(2,128)(2,1)S(1)} fusion(f32[4,4,1,1,1]{1,2,0,4,3:T(1,128)S(1)} %bitcast.304, bf16[2,4,4,64,256]{4,3,2,1,0:T(8,128)(2,1)S(1)} %bitcast.261), kind=kOutput, calls=%fused_computation.82 | convolution fusion | flops 6291456 | bytes 1114176 | tf_op jit(solution)/shard_map/ab,qcabkl->qckl/dot_general | solution.py:117
  101.8 1.3 %fusion.145 = bf16[1,2,2,256,256]{4,0,3,2,1:T(2,128)(2,1)S(1)} fusion(bf16[2,2,2,256,256]{4,0,3,2,1:T(2,128)(2,1)S(1)} %copy.12, s32[]{:T(128)S(1)} %bitcast.305, s32[]{:T(128)S(6)} %mul.205), kind=kOutput, calls=%fused_computation.194 | convolution fusion | flops 1048580 | bytes 1572872 | tf_op jit(solution)/shard_map/qt,tmcij->qmcij/dot_general | solution.py:63
  103.0 0.1 copy.37
  103.1 13.8 %all-gather = bf16[2,256,256]{2,1,0:T(8,128)(2,1)S(1)} all-gather(bf16[2,64,256]{2,1,0:T(8,128)(2,1)S(1)} %bitcast.271), channel_id=2, replica_groups=mesh['ens'=2,'space'=4,'tm'=2,'mom'=2] {'space'}, dimensions={1}, use_global_device_ids=true | all-gather | bytes 327680 | tf_op jit(solution)/shard_map/all_gather | solution.py:123
  116.9 0.0 all-to-all-done
  116.9 0.5 reduce_sum.14
  117.5 0.2 fusion.100
  117.7 0.3 fusion.99
  118.0 0.3 fusion.20
  118.3 0.3 fusion.19
  118.5 0.2 fusion.135
  118.7 0.2 fusion.134
  118.9 0.2 fusion.40
  119.2 0.2 fusion.39
  119.4 0.7 copy.20
  (14 shorter events, 0.3 us)
Async XLA Ops:
  0.0 99.6 %copy-start = (bf16[1,2,4,4,64,256]{5,4,3,2,1,0:T(8,128)(2,1)S(1)}, bf16[1,2,4,4,64,256]{5,4,3,2,1,0:T(8,128)(2,1)}, u32[]{:S(2)}) copy-start(bf16[1,2,4,4,64,256]{5,4,3,2,1,0:T(8,128)(2,1)} %param.9) | copy-start | bytes 3145732
  1.3 2.6 %copy-start.1 = (bf16[2,2,3,256,512]{4,3,2,1,0:T(8,128)(2,1)S(1)}, bf16[2,2,3,256,512]{4,3,2,1,0:T(8,128)(2,1)}, u32[]{:S(2)}) copy-start(bf16[2,2,3,256,512]{4,3,2,1,0:T(8,128)(2,1)} %param.5) | copy-start | bytes 9437188
  90.5 2.6 %copy-start.3 = (s32[2,2]{1,0:T(2,128)S(1)}, s32[2,2]{1,0:T(2,128)}, u32[]{:S(2)}) copy-start(s32[2,2]{1,0:T(2,128)} %param.7) | copy-start | bytes 52
  95.7 3.9 %copy-start.2 = (f32[4,4]{1,0:T(4,128)S(1)}, f32[4,4]{1,0:T(4,128)}, u32[]{:S(2)}) copy-start(f32[4,4]{1,0:T(4,128)} %param.8) | copy-start | bytes 196
  95.7 21.2 %all-to-all-start = ((bf16[2,1,2,2,256,256]{5,4,3,2,1,0:T(8,128)(2,1)}), bf16[2,1,2,2,256,256]{5,4,3,2,1,0:T(8,128)(2,1)S(1)}, u32[]{:S(2)}, u32[]{:S(2)}) async-start(bf16[2,1,2,2,256,256]{5,4,3,2,1,0:T(8,128)(2,1)} %copy.13), calls=%async_computation | async-start | bytes 2097152 | tf_op jit(solution)/shard_map/all_to_all | solution.py:113
where the time goes:
time: 120 us
  blocking collectives  93.1 us (78%)
  matrix products  15.5 us (13%)
  local copies, waits for them, and re-layouts  5.32 us (4%)
  starting transfers between devices  3.89 us (3%)
  other arithmetic  1.86 us (2%)
    psum x1, blocking collectives, local(): whole = lax.psum(partial_value, 'space').astype(jnp.bfloat16)  79.3 us
    all_gather x1, blocking collectives, local(): lax.all_gather(mixed_peramb, 'space', axis=2, tiled=True)  13.8 us
    all_to_all x1, starting transfers between devices, local(): lax.all_to_all(outgoing, 'tm', split_axis=0, concat_axis=0, tiled=True)  3.89 us
    dot_general x4, matrix products, elemental_terms(): lax.dot_general(imag_vec, imag_turned, contract_dims, preferred_element_t...  3.57 us
    convert_element_type x1, local copies, waits for them, and re-layouts, local(): whole = lax.psum(partial_value, 'space').astype(jnp.bfloat16)  2.54 us
  transfers between devices with their start and end apart: 1, of which 0 were waited for; matrix products, arithmetic and copies ran while one was open for 3% of the time, Pallas kernels for 0%

commit v1 on v0

--- a/solution.py
+++ b/solution.py
@@ -108,7 +108,7 @@
     cosine_rows, sine_rows = phases(momenta, site_ids)
     partial_value = elemental_terms(eigvecs, cosine_rows, sine_rows)
     my_pairs = lax.dynamic_slice_in_dim(pairs, my_group * pair_dev, pair_dev, 0)
-    whole = lax.psum(partial_value, "space").astype(jnp.bfloat16)
+    whole = jnp.sum(lax.all_gather(partial_value, "space"), axis=0).astype(jnp.bfloat16)
     outgoing = source_slots(whole, pairs, my_group, times_dev, tm_size, pair_dev)
     arrived = lax.all_to_all(outgoing, "tm", split_axis=0, concat_axis=0, tiled=True)
     source_full = jnp.sum(arrived, axis=0, dtype=jnp.float32).astype(jnp.bfloat16)

time: 120 us -> 210 us (1.75)
  waiting for transfers between devices: 0.01 us -> 150 us
  blocking collectives: 93.1 us -> 14.3 us
  between operations: 0.38 us -> 13.8 us
  other arithmetic: 1.86 us -> 6.05 us
    all_gather x0 -> x1, waiting for transfers between devices: none -> 150 us  [local(): lax.all_gather(partial_value, 'space')]
    psum x1 -> x0, blocking collectives: 79.3 us -> none  [local(): whole = lax.psum(partial_value, 'space').astype(jnp.bfloat16)]
    reduce_sum x0 -> x1, other arithmetic: none -> 4.19 us  [local(): jnp.sum(lax.all_gather(partial_value, 'space'), axis=0).astype(jnp.bfloat16)]
  transfers between devices with their start and end apart: 1 -> 2, of which waited for: 0 -> 1; matrix products, arithmetic and copies ran while one was open for 3% -> 2% of each run, Pallas kernels for 0% -> 0%
where the time goes in v1:
time: 210 us
  waiting for transfers between devices  150 us (71%)
  matrix products  15.5 us (7%)
  blocking collectives  14.3 us (7%)
  between operations  13.8 us (7%)
  local copies, waits for them, and re-layouts  6.89 us (3%)
  other arithmetic  6.05 us (3%)
  starting transfers between devices  3.71 us (2%)
    all_gather x1, waiting for transfers between devices, local(): lax.all_gather(partial_value, 'space')  150 us
    all_gather x1, blocking collectives, local(): lax.all_gather(mixed_peramb, 'space', axis=2, tiled=True)  14.3 us
  transfers between devices with their start and end apart: 2, of which 1 were waited for; matrix products, arithmetic and copies ran while one was open for 2% of the time, Pallas kernels for 0%

profile of v1, /device:TPU:0, one launch (start us, length us, event | category | flops | bytes accessed | tf_op | source)
XLA Modules:
  0.0 209.8 jit_solution(2841178052176012010)
XLA Ops:
  6.5 0.0 copy-start
  6.5 0.0 all-gather.4.cloned.1.call-start
  6.6 0.8 convert_element_type.166
  7.3 0.2 slice_reduce_fusion.3
  7.5 0.1 fusion.149
  7.7 0.1 sin.3
  7.8 0.0 copy-start.3
  7.8 2.2 %convolution_bitcast_fusion.14 = f32[256,256]{1,0:T(8,128)S(1)} fusion(f32[512]{0:T(512)S(1)} %bitcast.290, f32[512]{0:T(512)S(1)} %bitcast.298, bf16[2,2,3,256,512]{4,3,2,1,0:T(8,128)(2,1)} %param.5), kind=kOutput, calls=%fused_computation.55 | convolution fusion | flops 203685888 | bytes 2625536 | tf_op jit(solution)/shard_map/dot_general | solution.py:38
  10.0 0.4 copy-done.3
  10.4 0.4 convolution_bitcast_fusion.12
  10.8 0.5 convolution_bitcast_fusion.10
  11.3 0.4 convolution_bitcast_fusion.8
  11.8 0.5 convolution_bitcast_fusion.6
  12.2 0.5 convolution_bitcast_fusion.4
  12.7 0.5 convolution_bitcast_fusion.2
  13.1 0.4 convolution_bitcast_fusion
  13.6 0.4 fusion.22
  14.0 0.5 fusion.24
  14.5 0.5 fusion.26
  15.0 0.5 fusion.28
  15.4 0.5 fusion.30
  15.9 0.5 fusion.32
  16.4 0.5 fusion.34
  16.8 0.5 fusion.36
  17.4 0.1 maximum_bitcast_fusion
  17.5 0.1 maximum_bitcast_fusion.1
  17.6 0.1 pad_maximum_fusion
  17.8 2.1 copy.11
  19.8 0.0 copy-start.4
  19.8 0.0 all-gather.4.cloned.1.call-update
  19.9 0.0 copy-start.5
  19.9 0.0 copy-done
  19.9 0.6 copy-done.4
  20.5 2.1 %fusion.41 = bf16[1,2,64,256,1]{3,0,4,2,1:T(2,128)(2,1)S(1)} fusion(f32[4,4,1,1,1]{1,2,0,4,3:T(1,128)S(1)} %bitcast.306, bf16[2,4,4,64,256]{4,3,2,1,0:T(8,128)(2,1)S(1)} %bitcast.262), kind=kOutput, calls=%fused_computation.82 | convolution fusion | flops 6291456 | bytes 1114176 | tf_op jit(solution)/shard_map/ab,qcabkl->qckl/dot_general | solution.py:117
  22.7 0.0 copy-done.5
  22.7 0.2 slice_reduce_fusion
  22.8 149.5 %all-gather.4.cloned.1.call-done = f32[8,2,2,256,256]{4,3,2,1,0:T(8,128)} async-done(((f32[2,2,2,256,256]{4,3,2,1,0:T(8,128)}), f32[8,2,2,256,256]{4,3,2,1,0:T(8,128)}) %all-gather.4.cloned.1.call-update) | async-done | bytes 8388624 | tf_op jit(solution)/shard_map/all_gather | solution.py:111
  172.3 4.2 %reduce_sum.23 = bf16[2,2,2,256,256]{4,3,2,1,0:T(8,128)(2,1)S(1)} reduce(f32[4,2,2,2,256,256]{5,4,3,2,1,0:T(8,128)} %bitcast.263, f32[]{:T(128)} %constant.49.clone.1), dimensions={0}, to_apply=%region_0.1 | reduce | flops 1572864 | bytes 9437188 | tf_op jit(solution)/shard_map/reduce_sum | solution.py:111
  176.5 0.5 copy.32
  177.1 0.9 copy.13
  178.0 0.0 copy-start.1
  178.0 1.3 fusion.16
  179.3 0.0 copy-done.1
  179.3 1.1 copy.14
  180.4 0.0 copy-start.2
  180.4 3.7 %all-to-all-start = ((bf16[2,1,2,2,256,256]{5,4,3,2,1,0:T(8,128)(2,1)}), bf16[2,1,2,2,256,256]{5,4,3,2,1,0:T(8,128)(2,1)S(1)}, u32[]{:S(2)}, u32[]{:S(2)}) async-start(bf16[2,1,2,2,256,256]{5,4,3,2,1,0:T(8,128)(2,1)} %copy.14), calls=%async_computation | async-start | bytes 2097152 | tf_op jit(solution)/shard_map/all_to_all | solution.py:113
  184.1 14.3 %all-gather.1 = bf16[2,256,256]{2,1,0:T(8,128)(2,1)S(1)} all-gather(bf16[2,64,256]{2,1,0:T(8,128)(2,1)S(1)} %bitcast.273), channel_id=3, replica_groups=mesh['ens'=2,'space'=4,'tm'=2,'mom'=2] {'space'}, dimensions={1}, use_global_device_ids=true | all-gather | bytes 327680 | tf_op jit(solution)/shard_map/all_gather | solution.py:123
  198.5 0.0 copy-done.2
  198.5 1.3 fusion.145
  199.7 0.1 copy.39
  199.9 0.0 all-to-all-done
  199.9 0.5 reduce_sum.24
  200.4 0.2 fusion.100
  200.6 0.3 fusion.99
  200.9 0.3 fusion.20
  201.2 0.3 fusion.19
  201.5 0.2 fusion.135
  201.7 0.2 fusion.134
  201.9 0.2 fusion.40
  202.1 0.2 fusion.39
  202.3 0.7 copy.21
  (14 shorter events, 0.3 us)
Async XLA Ops:
  6.5 13.3 %copy-start = (bf16[1,2,4,4,64,256]{5,4,3,2,1,0:T(8,128)(2,1)S(1)}, bf16[1,2,4,4,64,256]{5,4,3,2,1,0:T(8,128)(2,1)}, u32[]{:S(2)}) copy-start(bf16[1,2,4,4,64,256]{5,4,3,2,1,0:T(8,128)(2,1)} %param.9) | copy-start | bytes 3145732
  6.5 165.8 %all-gather.4.cloned.1.call-start = ((), (), s32[]{:S(2)}) async-start(), calls=%async_computation.1 | async-start | bytes 10485760 | tf_op jit(solution)/shard_map/all_gather | solution.py:111
  7.8 2.6 %copy-start.3 = (bf16[2,2,3,256,512]{4,3,2,1,0:T(8,128)(2,1)S(1)}, bf16[2,2,3,256,512]{4,3,2,1,0:T(8,128)(2,1)}, u32[]{:S(2)}) copy-start(bf16[2,2,3,256,512]{4,3,2,1,0:T(8,128)(2,1)} %param.5) | copy-start | bytes 9437188
  19.8 0.7 copy-start.4
  19.9 2.8 %copy-start.5 = (s32[2,2]{1,0:T(2,128)S(1)}, s32[2,2]{1,0:T(2,128)}, u32[]{:S(2)}) copy-start(s32[2,2]{1,0:T(2,128)} %param.7) | copy-start | bytes 52
  178.0 1.3 copy-start.1
  180.4 18.0 %copy-start.2 = (bf16[2,2,2,256,256]{4,0,3,2,1:T(2,128)(2,1)S(1)}, bf16[2,2,2,256,256]{4,0,3,2,1:T(2,128)(2,1)}, u32[]{:S(2)}) copy-start(bf16[2,2,2,256,256]{4,0,3,2,1:T(2,128)(2,1)} %copy-done.1) | copy-start | bytes 3145732
  180.4 19.4 %all-to-all-start = ((bf16[2,1,2,2,256,256]{5,4,3,2,1,0:T(8,128)(2,1)}), bf16[2,1,2,2,256,256]{5,4,3,2,1,0:T(8,128)(2,1)S(1)}, u32[]{:S(2)}, u32[]{:S(2)}) async-start(bf16[2,1,2,2,256,256]{5,4,3,2,1,0:T(8,128)(2,1)} %copy.14), calls=%async_computation | async-start | bytes 2097152 | tf_op jit(solution)/shard_map/all_to_all | solution.py:113
Sparse Core Ops, SparseCore 0:
  20.0 152.3 all-gather.3
